TPU v7x, 128 devices: a whole 4x4x4 slice. The times are simulated.
128 devices in a mesh: prow: 8 (over y, core), pcol: 16 (over x, z).
Axes of the slice: x: 4, y: 4, z: 4, core: 2. Of those that a mesh axis runs over, the one named last changes fastest.
Arguments:
- cross_cov: float32 [2, 512, 16384], P(None, 'prow', 'pcol'), may hold values from -6 to 6
- prev_rows: bfloat16 [2, 512, 32768], P(None, 'pcol', 'prow'), may hold values from -0.046875 to 0.046875
- prev_solved: bfloat16 [32768, 16384], P('prow', 'pcol'), may hold values from -6 to 6
- sub_block: float32 [512, 512], replicated, may hold values from -0.25 to 0.25
- inv_first: float32 [512, 512], replicated, as said below
- inv_second: float32 [512, 512], replicated, as said below
Outputs:
- solved: float32 [2, 512, 16384], P(None, 'prow', 'pcol')
Inputs may be any that keep to these rules, and one draw needn't show every extreme that they name: inv_first is lower triangular with a positive diagonal. inv_second is lower triangular with a positive diagonal.
All inputs are finite; a program needn't handle non-finite values.
Results may differ from a plain program's by a relative error of at most 0.0003.
Values may be sent and summed in bfloat16 or wider, within the bound.
A program may use at most 64 MiB of HBM per device.

v0:
```python
import jax
import jax.numpy as jnp
from jax import lax
from jax.sharding import PartitionSpec as P


def mult(left, right, precision=lax.Precision.HIGHEST):
    return jnp.dot(left, right, preferred_element_type=jnp.float32, precision=precision)


def local(cross_cov, prev_rows, prev_solved, sub_block, inv_first, inv_second):
    rows = cross_cov.shape[1]
    pieces = 2
    width = prev_rows.shape[2] // pieces
    terms = None
    for p in range(pieces):
        gathered = lax.all_gather(
            prev_rows[:, :, p * width : (p + 1) * width], "pcol", axis=1, tiled=True
        )
        part = jnp.einsum(
            "kra,ac->krc",
            gathered,
            prev_solved[p * width : (p + 1) * width],
            preferred_element_type=jnp.float32,
        )
        terms = part if terms is None else terms + part
    offset = lax.axis_index("prow") * rows
    rhs = lax.dynamic_update_slice_in_dim(
        -terms, lax.dynamic_slice_in_dim(-terms, offset, rows, 1) + cross_cov, offset, 1
    )
    coupling = -mult(inv_second, mult(sub_block, inv_first))
    high = lax.Precision.HIGH
    nb = inv_first.shape[0]
    transform = jnp.concatenate(
        [
            jnp.concatenate([inv_first, jnp.zeros_like(inv_first)], axis=1),
            jnp.concatenate([coupling, inv_second], axis=1),
        ]
    )
    flat = rhs.reshape(2 * nb, -1)
    cols = flat.shape[1] // pieces
    out = []
    for p in range(pieces):
        both = mult(transform, flat[:, p * cols : (p + 1) * cols], high).reshape(2, nb, cols)
        out.append(lax.psum_scatter(both, "prow", scatter_dimension=1, tiled=True))
    return jnp.concatenate(out, axis=2)


def solution(mesh):
    return jax.shard_map(
        local,
        mesh=mesh,
        in_specs=(
            P(None, "prow", "pcol"),
            P(None, "pcol", "prow"),
            P("prow", "pcol"),
            P(),
            P(),
            P(),
        ),
        out_specs=P(None, "prow", "pcol"),
        check_vma=False,
    )
```

profile of v0, /device:TPU:0, one launch (start us, length us, event | category | flops | bytes accessed | tf_op | source)
XLA Modules:
  0.0 208.2 jit_solution(16049799425421940616)
XLA Ops:
  6.5 0.0 copy-start
  6.5 2.0 fusion.23
  8.6 0.0 all-gather.5.cloned.1.call-update
  8.6 0.0 all-gather.3.cloned.1.call-start
  8.7 0.7 all-gather.3.cloned.1.call-update
  9.4 0.0 reduce-scatter.5.cloned.1.call-start
  9.4 2.5 %copy.7 = f32[512,512]{0,1:T(8,128)} copy(f32[512,512]{1,0:T(8,128)} %param.10) | data formatting | bytes 2097152 | tf_op args[4]
  12.0 1.4 copy.8
  13.4 0.0 copy-done
  13.4 1.9 fusion.24
  15.2 3.5 %fusion.16 = f32[512,512]{0,1:T(8,128)S(1)} fusion(f32[512,512]{1,0:T(8,128)S(1)} %fusion.24, f32[512,512]{1,0:T(8,128)S(1)} %copy-done.2), kind=kOutput, calls=%fused_computation.18 | convolution fusion | flops 1610874880 | bytes 3145728 | tf_op jit(solution)/shard_map/dot_general | solution.py:8
  18.7 45.1 %all-gather.5.cloned.1.call-done = bf16[2,512,2048]{2,1,0:T(8,128)(2,1)} async-done(((bf16[2,32,2048]{2,1,0:T(8,128)(2,1)}), bf16[2,512,2048]{2,1,0:T(8,128)(2,1)}) %all-gather.5.cloned.1.call-update) | async-done | bytes 4194320 | tf_op jit(solution)/shard_map/all_gather | solution.py:17
  63.8 9.9 %fusion = f32[2,512,1024]{2,1,0:T(8,128)} fusion(bf16[2,512,2048]{2,1,0:T(8,128)(2,1)} %all-gather.5.cloned.1.call-done, bf16[4096,1024]{1,0:T(8,128)(2,1)} %param.8), kind=kOutput, calls=%fused_computation.2 | convolution fusion | flops 4294967296 | bytes 12582912 | tf_op jit(solution)/shard_map/kra,ac->krc/dot_general | solution.py:20
  73.7 43.6 %all-gather.3.cloned.1.call-done = bf16[2,512,2048]{2,1,0:T(8,128)(2,1)} async-done(((bf16[2,32,2048]{2,1,0:T(8,128)(2,1)}), bf16[2,512,2048]{2,1,0:T(8,128)(2,1)}) %all-gather.3.cloned.1.call-update) | async-done | bytes 4194320 | tf_op jit(solution)/shard_map/all_gather | solution.py:17
  117.3 9.2 %add_negate_fusion = f32[2,512,1024]{2,1,0:T(8,128)S(1)} fusion(f32[2,512,1024]{2,1,0:T(8,128)} %fusion, bf16[2,512,2048]{2,1,0:T(8,128)(2,1)} %all-gather.3.cloned.1.call-done, bf16[4096,1024]{1,0:T(8,128)(2,1)} %param.8), kind=kOutput, calls=%fused_computation.6 | convolution fusion | flops 4297064448 | bytes 16777216 | tf_op jit(solution)/shard_map/kra,ac->krc/dot_general | solution.py:20
  126.5 0.1 add_dynamic-update-slice_fusion
  126.7 5.1 %fusion.6 = f32[1024,512]{1,0:T(8,128)} fusion(f32[512,512]{0,1:T(8,128)S(1)} %copy-done.3, f32[512,512]{0,1:T(8,128)S(1)} %copy-done.4, f32[512,512]{0,1:T(8,128)S(1)} %fusion.16, f32[1024,1024]{1,0:T(8,128)S(1)} %bitcast.21), kind=kOutput, calls=%fused_computation.9 | convolution fusion | flops 3225419776 | bytes 7340032 | tf_op jit(solution)/shard_map/dot_general | solution.py:8
  131.8 0.0 reduce-scatter.5.cloned.1.call-update
  131.8 0.0 reduce-scatter.3.cloned.1.call-start
  131.8 6.7 %fusion.7 = f32[1024,512]{1,0:T(8,128)} fusion(f32[512,512]{0,1:T(8,128)S(1)} %copy-done.3, f32[512,512]{0,1:T(8,128)} %copy.8, f32[512,512]{0,1:T(8,128)S(1)} %fusion.16, f32[1024,1024]{1,0:T(8,128)} %bitcast.22), kind=kOutput, calls=%fused_computation.10 | convolution fusion | flops 3225419776 | bytes 7340032 | tf_op jit(solution)/shard_map/dot_general | solution.py:8
  138.6 0.0 reduce-scatter.3.cloned.1.call-update
  138.6 26.6 %reduce-scatter.5.cloned.1.call-done = f32[2,64,512]{2,1,0:T(8,128)} async-done(((f32[2,512,512]{2,1,0:T(8,128)}), f32[2,64,512]{2,1,0:T(8,128)}) %reduce-scatter.5.cloned.1.call-update) | async-done | bytes 262160 | tf_op jit(solution)/shard_map/reduce_scatter | solution.py:45
  165.2 34.7 %reduce-scatter.3.cloned.1.call-done = f32[2,64,512]{2,1,0:T(8,128)} async-done(((f32[2,512,512]{2,1,0:T(8,128)}), f32[2,64,512]{2,1,0:T(8,128)}) %reduce-scatter.3.cloned.1.call-update) | async-done | bytes 262160 | tf_op jit(solution)/shard_map/reduce_scatter | solution.py:45
  199.8 1.9 pad_maximum_fusion
  (13 shorter events, 0.0 us)
Async XLA Ops:
  6.5 6.8 %copy-start = (f32[512,512]{1,0:T(8,128)S(1)}, f32[512,512]{1,0:T(8,128)}, u32[]{:S(2)}) copy-start(f32[512,512]{1,0:T(8,128)} %param.9) | copy-start | bytes 3145732
  6.5 6.8 %copy-start.1 = (f32[512,512]{1,0:T(8,128)S(1)}, f32[512,512]{1,0:T(8,128)}, u32[]{:S(2)}) copy-start(f32[512,512]{1,0:T(8,128)} %param.10) | copy-start | bytes 3145732
  6.5 5.4 %copy-start.2 = (f32[512,512]{1,0:T(8,128)S(1)}, f32[512,512]{1,0:T(8,128)}, u32[]{:S(2)}) copy-start(f32[512,512]{1,0:T(8,128)} %param.11) | copy-start | bytes 3145732
  6.5 57.2 %all-gather.5.cloned.1.call-start = ((), (), s32[]{:S(2)}) async-start(), calls=%async_computation.3 | async-start | bytes 4456448 | tf_op jit(solution)/shard_map/all_gather | solution.py:17
  8.6 108.6 %all-gather.3.cloned.1.call-start = ((), (), s32[]{:S(2)}) async-start(), calls=%async_computation.2 | async-start | bytes 4456448 | tf_op jit(solution)/shard_map/all_gather | solution.py:17
  9.4 155.8 %reduce-scatter.5.cloned.1.call-start = ((), (), s32[]{:S(2)}) async-start(), calls=%async_computation.5 | async-start | bytes 2359296 | tf_op jit(solution)/shard_map/reduce_scatter | solution.py:45
  73.7 53.0 %copy-start.3 = (f32[512,512]{0,1:T(8,128)S(1)}, f32[512,512]{0,1:T(8,128)}, u32[]{:S(2)}) copy-start(f32[512,512]{0,1:T(8,128)} %copy.7) | copy-start | bytes 3145732
  117.3 9.3 %copy-start.5 = (f32[2,64,1024]{2,1,0:T(8,128)S(1)}, f32[2,64,1024]{2,1,0:T(8,128)}, u32[]{:S(2)}) copy-start(f32[2,64,1024]{2,1,0:T(8,128)} %param.6) | copy-start | bytes 1572868
  117.3 9.4 %copy-start.4 = (f32[512,512]{0,1:T(8,128)S(1)}, f32[512,512]{0,1:T(8,128)}, u32[]{:S(2)}) copy-start(f32[512,512]{0,1:T(8,128)} %copy.8) | copy-start | bytes 3145732
  126.6 5.1 %copy-start.6 = (f32[2,512,1024]{2,1,0:T(8,128)}, f32[2,512,1024]{2,1,0:T(8,128)S(1)}, u32[]{:S(2)}) copy-start(f32[2,512,1024]{2,1,0:T(8,128)S(1)} %add_dynamic-update-slice_fusion) | copy-start | bytes 12582916
  131.8 68.1 %reduce-scatter.3.cloned.1.call-start = ((), (), s32[]{:S(2)}) async-start(), calls=%async_computation.4 | async-start | bytes 2359296 | tf_op jit(solution)/shard_map/reduce_scatter | solution.py:45
Sparse Core Ops, SparseCore 0:
  9.6 54.1 all-gather.4
  66.0 51.2 all-gather.2
  131.9 33.2 reduce-scatter.4
  167.4 32.3 reduce-scatter.2
where the time goes:
time: 208 us
  waiting for transfers between devices  151 us (73%)
  matrix products  36.3 us (17%)
  between operations  13.2 us (6%)
  local copies, waits for them, and re-layouts  6 us (3%)
    all_gather x2, waiting for transfers between devices, local(): lax.all_gather(prev_rows[:, :, p * width:(p + 1) * width], 'pcol', axis=1...  88.6 us
    reduce_scatter x2, waiting for transfers between devices, local(): out.append(lax.psum_scatter(both, 'prow', scatter_dimension=1, tiled=True))  61.2 us
    dot_general x2, matrix products, local(): jnp.einsum('kra,ac->krc', gathered, prev_solved[p * width:(p + 1) * width...  19.2 us
    dot_general x4, matrix products, mult(): jnp.dot(left, right, preferred_element_type=jnp.float32, precision=precis...  17.1 us
  transfers between devices with their start and end apart: 4, of which 4 were waited for; matrix products, arithmetic and copies ran while one was open for 12% of the time, Pallas kernels for 0%

commit v1 on v0

--- a/solution.py
+++ b/solution.py
@@ -14,8 +14,14 @@
     width = prev_rows.shape[2] // pieces
     terms = None
     for p in range(pieces):
-        gathered = lax.all_gather(
-            prev_rows[:, :, p * width : (p + 1) * width], "pcol", axis=1, tiled=True
+        gathered = jnp.concatenate(
+            lax.all_to_all(
+                jnp.stack([prev_rows[:, :, p * width : (p + 1) * width]] * lax.axis_size("pcol")),
+                "pcol",
+                0,
+                0,
+            ),
+            axis=1,
         )
         part = jnp.einsum(
             "kra,ac->krc",

time: 208 us -> 224 us (1.077)
  blocking collectives: 0 us -> 58.6 us
  waiting for transfers between devices: 151 us -> 104 us
  matrix products: 36.3 us -> 28 us
  local copies, waits for them, and re-layouts: 6 us -> 12.6 us
  starting transfers between devices: 0.12 us -> 4.75 us
    all_gather x2 -> x0, waiting for transfers between devices: 88.6 us -> none  [local(): lax.all_gather(prev_rows[:, :, p * width:(p + 1) * width], 'pcol', axis=1...]
    all_to_all x0 -> x1, blocking collectives: none -> 58.6 us  [local(): lax.all_to_all(jnp.stack([prev_rows[:, :, p * width:(p + 1) * width]] * l...]
    all_to_all x0 -> x1, waiting for transfers between devices: none -> 43.9 us  [local(): lax.all_to_all(jnp.stack([prev_rows[:, :, p * width:(p + 1) * width]] * l...]
    dot_general x2, matrix products: 19.2 us -> 11 us  [local(): jnp.einsum('kra,ac->krc', gathered, prev_solved[p * width:(p + 1) * width...]
    reshape x0 -> x2, local copies, waits for them, and re-layouts: none -> 4.94 us  [local(): jnp.concatenate(lax.all_to_all(jnp.stack([prev_rows[:, :, p * width:(p +...]
    all_to_all x0 -> x1, starting transfers between devices: none -> 4.67 us  [local(): lax.all_to_all(jnp.stack([prev_rows[:, :, p * width:(p + 1) * width]] * l...]
    another operation x0 -> x2, local copies, waits for them, and re-layouts: none -> 3.02 us  [local(): jnp.stack([prev_rows[:, :, p * width:(p + 1) * width]] * lax.axis_size('p...]
  transfers between devices with their start and end apart: 4 -> 3, of which waited for: 4 -> 3; matrix products, arithmetic and copies ran while one was open for 12% -> 8% of each run, Pallas kernels for 0% -> 0%
where the time goes in v1:
time: 224 us
  waiting for transfers between devices  104 us (46%)
  blocking collectives  58.6 us (26%)
  matrix products  28 us (12%)
  between operations  13.6 us (6%)
  local copies, waits for them, and re-layouts  12.6 us (6%)
  starting transfers between devices  4.75 us (2%)
    reduce_scatter x2, waiting for transfers between devices, local(): out.append(lax.psum_scatter(both, 'prow', scatter_dimension=1, tiled=True))  60.2 us
    all_to_all x1, blocking collectives, local(): lax.all_to_all(jnp.stack([prev_rows[:, :, p * width:(p + 1) * width]] * l...  58.6 us
    all_to_all x1, waiting for transfers between devices, local(): lax.all_to_all(jnp.stack([prev_rows[:, :, p * width:(p + 1) * width]] * l...  43.9 us
    dot_general x4, matrix products, mult(): jnp.dot(left, right, preferred_element_type=jnp.float32, precision=precis...  17 us
    dot_general x2, matrix products, local(): jnp.einsum('kra,ac->krc', gathered, prev_solved[p * width:(p + 1) * width...  11 us
    reshape x2, local copies, waits for them, and re-layouts, local(): jnp.concatenate(lax.all_to_all(jnp.stack([prev_rows[:, :, p * width:(p +...  4.94 us
    all_to_all x1, starting transfers between devices, local(): lax.all_to_all(jnp.stack([prev_rows[:, :, p * width:(p + 1) * width]] * l...  4.67 us
  transfers between devices with their start and end apart: 3, of which 3 were waited for; matrix products, arithmetic and copies ran while one was open for 8% of the time, Pallas kernels for 0%

profile of v1, /device:TPU:0, one launch (start us, length us, event | category | flops | bytes accessed | tf_op | source)
XLA Modules:
  0.0 223.6 jit_solution(11536130434926452560)
XLA Ops:
  6.5 1.2 fusion.23
  7.7 0.5 stack.5
  8.2 58.6 %all_to_all.10 = bf16[16,2,32,2048]{3,2,1,0:T(8,128)(2,1)} all-to-all(bf16[16,2,32,2048]{3,2,1,0:T(8,128)(2,1)S(1)} %stack.5), channel_id=1, replica_groups=mesh['prow'=8,'pcol'=16] {'pcol'}, dimensions={0} | all-to-all | bytes 8388608 | tf_op jit(solution)/shard_map/all_to_all | solution.py:18
  66.8 2.5 %stack.4 = bf16[16,2,32,2048]{3,2,1,0:T(8,128)(2,1)} broadcast(bf16[2,32,2048]{2,1,0:T(8,128)(2,1)S(1)} %get-tuple-element.5), dimensions={1,2,3} | broadcast | bytes 4456448 | tf_op jit(solution)/shard_map/stack | solution.py:19
  69.3 4.7 %all-to-all-start = ((bf16[16,2,32,2048]{3,2,1,0:T(8,128)(2,1)}), bf16[16,2,32,2048]{3,2,1,0:T(8,128)(2,1)}, u32[]{:S(2)}, u32[]{:S(2)}) async-start(bf16[16,2,32,2048]{3,2,1,0:T(8,128)(2,1)} %stack.4), calls=%async_computation | async-start | bytes 8388608 | tf_op jit(solution)/shard_map/all_to_all | solution.py:18
  74.0 0.0 reduce-scatter.3.cloned.1.call-start
  74.1 1.3 copy.10
  75.4 1.4 copy.9
  76.8 1.8 fusion.24
  78.6 3.5 %fusion.16 = f32[512,512]{0,1:T(8,128)S(1)} fusion(f32[512,512]{1,0:T(8,128)S(1)} %fusion.24, f32[512,512]{1,0:T(8,128)S(1)} %copy-done.3), kind=kOutput, calls=%fused_computation.18 | convolution fusion | flops 1610874880 | bytes 3145728 | tf_op jit(solution)/shard_map/dot_general | solution.py:8
  82.1 2.3 %copy.12 = bf16[2,16,32,2048]{3,2,1,0:T(8,128)(2,1)} copy(bf16[2,16,32,2048]{3,2,0,1:T(8,128)(2,1)S(1)} %bitcast.23) | data formatting | bytes 8388608 | tf_op jit(solution)/shard_map/reshape | solution.py:17
  84.4 43.9 %all-to-all-done = bf16[16,2,32,2048]{3,2,1,0:T(8,128)(2,1)} async-done(((bf16[16,2,32,2048]{3,2,1,0:T(8,128)(2,1)}), bf16[16,2,32,2048]{3,2,1,0:T(8,128)(2,1)}, u32[]{:S(2)}, u32[]{:S(2)}) %all-to-all-start) | async-done | bytes 4194336 | tf_op jit(solution)/shard_map/all_to_all | solution.py:18
  128.3 2.7 %copy.11 = bf16[2,16,32,2048]{3,2,1,0:T(8,128)(2,1)S(1)} copy(bf16[2,16,32,2048]{3,2,0,1:T(8,128)(2,1)} %bitcast.1) | data formatting | bytes 8388608 | tf_op jit(solution)/shard_map/reshape | solution.py:17
  130.9 0.8 copy-done.4
  131.7 6.5 %fusion = f32[2,512,1024]{2,1,0:T(8,128)S(1)} fusion(bf16[2,512,2048]{2,1,0:T(8,128)(2,1)S(1)} %bitcast.24, bf16[4096,1024]{1,0:T(8,128)(2,1)} %param.8), kind=kOutput, calls=%fused_computation.2 | convolution fusion | flops 4294967296 | bytes 12582912 | tf_op jit(solution)/shard_map/kra,ac->krc/dot_general | solution.py:26
  138.3 4.5 %add_negate_fusion = f32[2,512,1024]{2,1,0:T(8,128)S(1)} fusion(f32[2,512,1024]{2,1,0:T(8,128)S(1)} %fusion, bf16[2,512,2048]{2,1,0:T(8,128)(2,1)S(1)} %bitcast.25, bf16[4096,1024]{1,0:T(8,128)(2,1)S(1)} %bitcast.31), kind=kOutput, calls=%fused_computation.6 | convolution fusion | flops 4297064448 | bytes 16777216 | tf_op jit(solution)/shard_map/kra,ac->krc/dot_general | solution.py:26
  142.9 0.1 add_dynamic-update-slice_fusion
  143.0 4.9 %fusion.7 = f32[1024,512]{1,0:T(8,128)} fusion(f32[512,512]{0,1:T(8,128)S(1)} %copy-done.6, f32[512,512]{0,1:T(8,128)S(1)} %copy-done.5, f32[512,512]{0,1:T(8,128)S(1)} %fusion.16, f32[1024,1024]{1,0:T(8,128)S(1)} %bitcast.28), kind=kOutput, calls=%fused_computation.10 | convolution fusion | flops 3225419776 | bytes 7340032 | tf_op jit(solution)/shard_map/dot_general | solution.py:8
  147.9 0.0 reduce-scatter.3.cloned.1.call-update
  148.0 0.0 reduce-scatter.5.cloned.1.call-start
  148.0 6.7 %fusion.6 = f32[1024,512]{1,0:T(8,128)} fusion(f32[512,512]{0,1:T(8,128)} %copy.9, f32[512,512]{0,1:T(8,128)S(1)} %copy-done.5, f32[512,512]{0,1:T(8,128)S(1)} %fusion.16, f32[1024,1024]{1,0:T(8,128)} %bitcast.29), kind=kOutput, calls=%fused_computation.9 | convolution fusion | flops 3225419776 | bytes 7340032 | tf_op jit(solution)/shard_map/dot_general | solution.py:8
  154.8 25.3 %reduce-scatter.3.cloned.1.call-done = f32[2,64,512]{2,1,0:T(8,128)} async-done(((f32[2,512,512]{2,1,0:T(8,128)}), f32[2,64,512]{2,1,0:T(8,128)}) %reduce-scatter.3.cloned.1.call-update) | async-done | bytes 262160 | tf_op jit(solution)/shard_map/reduce_scatter | solution.py:51
  180.0 34.9 %reduce-scatter.5.cloned.1.call-done = f32[2,64,512]{2,1,0:T(8,128)} async-done(((f32[2,512,512]{2,1,0:T(8,128)}), f32[2,64,512]{2,1,0:T(8,128)}) %reduce-scatter.5.cloned.1.call-update) | async-done | bytes 262160 | tf_op jit(solution)/shard_map/reduce_scatter | solution.py:51
  214.9 1.9 pad_maximum_fusion
  (23 shorter events, 0.1 us)
Async XLA Ops:
  6.5 70.2 %copy-start = (f32[512,512]{1,0:T(8,128)S(1)}, f32[512,512]{1,0:T(8,128)}, u32[]{:S(2)}) copy-start(f32[512,512]{1,0:T(8,128)} %param.9) | copy-start | bytes 3145732
  69.3 4.7 %copy-start.3 = (f32[512,512]{1,0:T(8,128)S(1)}, f32[512,512]{1,0:T(8,128)}, u32[]{:S(2)}) copy-start(f32[512,512]{1,0:T(8,128)} %param.11) | copy-start | bytes 3145732
  69.3 6.0 %copy-start.2 = (f32[512,512]{1,0:T(8,128)S(1)}, f32[512,512]{1,0:T(8,128)}, u32[]{:S(2)}) copy-start(f32[512,512]{1,0:T(8,128)} %param.10) | copy-start | bytes 3145732
  69.3 59.0 %all-to-all-start = ((bf16[16,2,32,2048]{3,2,1,0:T(8,128)(2,1)}), bf16[16,2,32,2048]{3,2,1,0:T(8,128)(2,1)}, u32[]{:S(2)}, u32[]{:S(2)}) async-start(bf16[16,2,32,2048]{3,2,1,0:T(8,128)(2,1)} %stack.4), calls=%async_computation | async-start | bytes 8388608 | tf_op jit(solution)/shard_map/all_to_all | solution.py:18
  74.0 106.0 %reduce-scatter.3.cloned.1.call-start = ((), (), s32[]{:S(2)}) async-start(), calls=%async_computation.4 | async-start | bytes 2359296 | tf_op jit(solution)/shard_map/reduce_scatter | solution.py:51
  76.7 5.3 %copy-start.1 = (bf16[16,2,32,2048]{3,2,1,0:T(8,128)(2,1)S(1)}, bf16[16,2,32,2048]{3,2,1,0:T(8,128)(2,1)}, u32[]{:S(2)}) copy-start(bf16[16,2,32,2048]{3,2,1,0:T(8,128)(2,1)} %all_to_all.10) | copy-start | bytes 12582916
  128.3 3.4 %copy-start.4 = (bf16[2,16,32,2048]{3,2,1,0:T(8,128)(2,1)S(1)}, bf16[2,16,32,2048]{3,2,1,0:T(8,128)(2,1)}, u32[]{:S(2)}) copy-start(bf16[2,16,32,2048]{3,2,1,0:T(8,128)(2,1)} %copy.12) | copy-start | bytes 12582916
  128.3 10.0 %slice-start = ((s8[8388608]{0:T(1024)(128)(4,1)}), s8[4194304]{0:T(1024)(128)(4,1)S(1)}, s32[]{:S(2)}) async-start(s8[8388608]{0:T(1024)(128)(4,1)} %bitcast.30), calls=%async_computation.6 | async-start | bytes 8388608
  131.7 6.6 %slice-start.1 = ((s8[8388608]{0:T(1024)(128)(4,1)}), s8[4194304]{0:T(1024)(128)(4,1)S(1)}, s32[]{:S(2)}) async-start(s8[8388608]{0:T(1024)(128)(4,1)} %bitcast.30), calls=%async_computation.7 | async-start | bytes 8388608
  138.3 4.6 %copy-start.7 = (f32[2,64,1024]{2,1,0:T(8,128)S(1)}, f32[2,64,1024]{2,1,0:T(8,128)}, u32[]{:S(2)}) copy-start(f32[2,64,1024]{2,1,0:T(8,128)} %param.6) | copy-start | bytes 1572868
  138.3 4.7 %copy-start.5 = (f32[512,512]{0,1:T(8,128)S(1)}, f32[512,512]{0,1:T(8,128)}, u32[]{:S(2)}) copy-start(f32[512,512]{0,1:T(8,128)} %copy.10) | copy-start | bytes 3145732
  138.3 4.7 %copy-start.6 = (f32[512,512]{0,1:T(8,128)S(1)}, f32[512,512]{0,1:T(8,128)}, u32[]{:S(2)}) copy-start(f32[512,512]{0,1:T(8,128)} %copy.9) | copy-start | bytes 3145732
  143.0 5.0 %copy-start.8 = (f32[2,512,1024]{2,1,0:T(8,128)}, f32[2,512,1024]{2,1,0:T(8,128)S(1)}, u32[]{:S(2)}) copy-start(f32[2,512,1024]{2,1,0:T(8,128)S(1)} %add_dynamic-update-slice_fusion) | copy-start | bytes 12582916
  148.0 67.0 %reduce-scatter.5.cloned.1.call-start = ((), (), s32[]{:S(2)}) async-start(), calls=%async_computation.5 | async-start | bytes 2359296 | tf_op jit(solution)/shard_map/reduce_scatter | solution.py:51
Sparse Core Ops, SparseCore 0:
  148.1 31.8 reduce-scatter.2
  182.4 32.4 reduce-scatter.4
